TPU v7x, 256 devices: a whole 4x4x8 slice. The times are simulated.
256 devices in a mesh: prow: 32 (over z_hi, y, x), pcol: 8 (over z_lo, core).
Axes of the slice: x: 4, y: 4, z: 8 (z_hi: 2, z_lo: 4; z = z_hi * 4 + z_lo), core: 2. Of those that a mesh axis runs over, the one named last changes fastest.
Arguments:
- eigen_rows: float32 [1024, 229376], P(('pcol', 'prow')), may hold values from -6 to 6
- reflectors: float32 [229376, 512], P('prow', 'pcol'), may hold values from -0.375 to 0.375
- tfactors: float32 [2, 256, 256], replicated, may hold values from -0.01171875 to 0.01171875
Outputs:
- back_rows: float32 [1024, 229376], P('pcol', 'prow')
All inputs are finite; a program needn't handle non-finite values.
Results may differ from a plain program's by a relative error of at most 0.000084.
Values sent between devices are 32-bit elements; how exact they have to be, the bound alone decides.
No kernel may reach another device: no remote copies, remote signals or barrier semaphores. Data moves between devices by JAX's collectives and lax.ppermute only.
A program may use at most 128 MiB of HBM per device.

v0:
```python
import jax
import jax.numpy as jnp
from jax import lax
from jax.sharding import PartitionSpec as P


def upper_part(square):
    width = square.shape[0]
    rows = lax.broadcasted_iota(jnp.int32, (width, width), 0)
    cols = lax.broadcasted_iota(jnp.int32, (width, width), 1)
    return jnp.where(cols >= rows, square, jnp.zeros_like(square))


def matmul(left, right, precision=lax.Precision.HIGHEST):
    return jnp.dot(left, right, precision=precision, preferred_element_type=jnp.float32)


def sum_over_prow(values, members):
    slices = values.reshape((members, -1, 128))
    received = lax.all_to_all(slices, "prow", split_axis=0, concat_axis=0, tiled=True)
    total = jnp.sum(received, axis=0, keepdims=True)
    copies = jnp.broadcast_to(total, slices.shape)
    return lax.all_to_all(copies, "prow", split_axis=0, concat_axis=0, tiled=True)


def body(eigen_rows, reflectors, tfactors):
    members = lax.axis_size("prow")
    width = tfactors.shape[1]
    vectors = lax.all_gather(reflectors, "pcol", axis=1, tiled=True)
    rows = lax.all_to_all(eigen_rows, "prow", split_axis=1, concat_axis=0, tiled=True)
    count = rows.shape[0]
    first_tri = upper_part(tfactors[0])
    second_tri = upper_part(tfactors[1])
    fast = lax.Precision.HIGH
    projected = matmul(rows, vectors, fast)
    cross = matmul(vectors[:, width:].T, vectors[:, :width], fast)
    packed = jnp.concatenate([projected.reshape(members, -1), cross.reshape(members, -1)], axis=1)
    packed = sum_over_prow(packed, members).reshape(packed.shape)
    split = projected.size // members
    projected = packed[:, :split].reshape(count, 2 * width)
    cross = packed[:, split:].reshape(width, width)
    scaled_second = matmul(projected[:, width:], second_tri.T)
    first = projected[:, :width] - matmul(scaled_second, cross)
    scaled_first = matmul(first, first_tri.T)
    scaled = jnp.concatenate([scaled_first, scaled_second], axis=1)
    return rows - matmul(scaled, vectors.T, fast)


def solution(mesh):
    return jax.shard_map(
        body,
        mesh=mesh,
        in_specs=(P(("pcol", "prow"), None), P("prow", "pcol"), P()),
        out_specs=P("pcol", "prow"),
        check_vma=False,
    )
```

profile of v0, /device:TPU:32, one launch (start us, length us, event | category | flops | bytes accessed | tf_op | source)
XLA Modules:
  0.0 336.6 jit_solution(14484541034405303866)
XLA Ops:
  6.5 0.0 all-gather.2.cloned.1.call-start
  6.5 0.7 all-gather.2.cloned.1.call-update
  7.3 139.8 %all_to_all.29 = f32[4,32,7168]{2,0,1:T(4,128)} all-to-all(f32[4,32,7168]{2,0,1:T(4,128)} %bitcast.19), channel_id=1, replica_groups=mesh['prow'=32,'pcol'=8] {'prow'}, dimensions={1} | all-to-all | bytes 7340032 | tf_op jit(solution)/shard_map/all_to_all | solution.py:30
  147.0 5.3 %all_to_all.23 = f32[128,7168]{1,0:T(8,128)} reshape(f32[32,4,7168]{2,1,0:T(4,128)} %bitcast.18) | data formatting | bytes 7340032 | tf_op jit(solution)/shard_map/all_to_all | solution.py:30
  152.3 86.0 %all-gather.2.cloned.1.call-done = f32[7168,512]{0,1:T(8,128)} async-done(((f32[7168,64]{0,1:T(8,128)}), f32[7168,512]{0,1:T(8,128)}) %all-gather.2.cloned.1.call-update) | async-done | bytes 14680080 | tf_op jit(solution)/shard_map/all_gather | solution.py:29
  238.3 11.7 %fusion = f32[256,256]{1,0:T(8,128)S(1)} fusion(f32[7168,512]{0,1:T(8,128)} %all-gather.2.cloned.1.call-done), kind=kOutput, calls=%fused_computation.1 | convolution fusion | flops 2818572288 | bytes 14942208 | tf_op jit(solution)/shard_map/dot_general | solution.py:15
  250.0 11.8 %fusion.17 = f32[128,512]{1,0:T(8,128)S(1)} fusion(f32[128,7168]{1,0:T(8,128)} %all_to_all.23, f32[7168,512]{0,1:T(8,128)} %all-gather.2.cloned.1.call-done), kind=kOutput, calls=%fused_computation.24 | convolution fusion | flops 2818572288 | bytes 18612224 | tf_op jit(solution)/shard_map/dot_general | solution.py:15
  261.9 0.0 copy-start
  261.9 0.1 pad_maximum_fusion
  262.0 32.9 %all_to_all.30 = f32[32,32,128]{2,1,0:T(8,128)S(1)} all-to-all(f32[32,32,128]{2,1,0:T(8,128)S(1)} %pad_maximum_fusion), channel_id=1, replica_groups=mesh['prow'=32,'pcol'=8] {'prow'}, dimensions={0} | all-to-all | bytes 1048576 | tf_op jit(solution)/shard_map/all_to_all | solution.py:20
  294.9 0.1 broadcast_in_dim.2
  295.0 20.4 %all_to_all.31 = f32[32,32,128]{2,1,0:T(8,128)S(1)} all-to-all(f32[32,32,128]{2,1,0:T(8,128)S(1)} %broadcast_in_dim.2), channel_id=1, replica_groups=mesh['prow'=32,'pcol'=8] {'prow'}, dimensions={0} | all-to-all | bytes 1048576 | tf_op jit(solution)/shard_map/all_to_all | solution.py:23
  315.4 0.3 copy.7
  315.8 0.1 reshape.21
  315.9 0.0 copy-done
  315.9 0.4 fusion.7
  316.3 0.3 convolution_subtract_fusion.1
  316.6 0.4 fusion.6
  317.0 12.8 %convolution_subtract_fusion = f32[128,7168]{1,0:T(8,128)} fusion(f32[128,7168]{1,0:T(8,128)} %all_to_all.23, f32[7168,512]{0,1:T(8,128)} %all-gather.2.cloned.1.call-done, f32[128,256]{1,0:T(8,128)S(1)} %fusion.7, f32[128,256]{1,0:T(8,128)S(1)} %fusion.6), kind=kOutput, calls=%fused_computation | convolution fusion | flops 2819555328 | bytes 22282240 | tf_op jit(solution)/shard_map/dot_general | solution.py:15
  (5 shorter events, 0.2 us)
Async XLA Ops:
  6.5 231.8 %all-gather.2.cloned.1.call-start = ((), (), s32[]{:S(2)}) async-start(), calls=%async_computation.3 | async-start | bytes 16515072 | tf_op jit(solution)/shard_map/all_gather | solution.py:29
  261.9 54.0 %copy-start = (f32[2,256,256]{2,1,0:T(8,128)S(1)}, f32[2,256,256]{2,1,0:T(8,128)}, u32[]{:S(2)}) copy-start(f32[2,256,256]{2,1,0:T(8,128)} %param.5) | copy-start | bytes 1572868
Sparse Core Ops, SparseCore 0:
  9.1 229.0 all-gather.1
where the time goes:
time: 337 us
  blocking collectives  193 us (57%)
  waiting for transfers between devices  86.7 us (26%)
  matrix products  37.4 us (11%)
  between operations  13.5 us (4%)
  local copies, waits for them, and re-layouts  5.81 us (2%)
    all_to_all x1, blocking collectives, body(): lax.all_to_all(eigen_rows, 'prow', split_axis=1, concat_axis=0, tiled=True)  140 us
    all_gather x1, waiting for transfers between devices, body(): vectors = lax.all_gather(reflectors, 'pcol', axis=1, tiled=True)  86 us
    dot_general x6, matrix products, matmul(): jnp.dot(left, right, precision=precision, preferred_element_type=jnp.floa...  37.4 us
    all_to_all x1, blocking collectives, sum_over_prow(): lax.all_to_all(slices, 'prow', split_axis=0, concat_axis=0, tiled=True)  32.9 us
    all_to_all x1, blocking collectives, sum_over_prow(): lax.all_to_all(copies, 'prow', split_axis=0, concat_axis=0, tiled=True)  20.4 us
  transfers between devices with their start and end apart: 1, of which 1 were waited for; matrix products, arithmetic and copies ran while one was open for 0% of the time, Pallas kernels for 0%

commit v1 on v0

--- a/solution.py
+++ b/solution.py
@@ -26,7 +26,10 @@
 def body(eigen_rows, reflectors, tfactors):
     members = lax.axis_size("prow")
     width = tfactors.shape[1]
-    vectors = lax.all_gather(reflectors, "pcol", axis=1, tiled=True)
+    size = lax.axis_size("pcol")
+    blocks = jnp.stack([reflectors for _ in range(size)])
+    blocks = lax.all_to_all(blocks, "pcol", split_axis=0, concat_axis=0)
+    vectors = jnp.concatenate(blocks, axis=1)
     rows = lax.all_to_all(eigen_rows, "prow", split_axis=1, concat_axis=0, tiled=True)
     count = rows.shape[0]
     first_tri = upper_part(tfactors[0])

time: 337 us -> 512 us (1.52)
  waiting for transfers between devices: 86.7 us -> 310 us
  blocking collectives: 193 us -> 143 us
  between operations: 13.5 us -> 0.13 us
  local copies, waits for them, and re-layouts: 5.81 us -> 12.8 us
  starting transfers between devices: 0.01 us -> 5.49 us
    all_to_all x0 -> x1, waiting for transfers between devices: none -> 310 us  [body(): blocks = lax.all_to_all(blocks, 'pcol', split_axis=0, concat_axis=0)]
    all_gather x1 -> x0, waiting for transfers between devices: 86 us -> none  [body(): vectors = lax.all_gather(reflectors, 'pcol', axis=1, tiled=True)]
    all_to_all x1, blocking collectives: 140 us -> 101 us  [body(): lax.all_to_all(eigen_rows, 'prow', split_axis=1, concat_axis=0, tiled=True)]
    all_to_all x1, blocking collectives: 32.9 us -> 22.4 us  [sum_over_prow(): lax.all_to_all(slices, 'prow', split_axis=0, concat_axis=0, tiled=True)]
    another operation x0 -> x1, local copies, waits for them, and re-layouts: none -> 6.95 us  [body(): blocks = jnp.stack([reflectors for _ in range(size)])]
    all_to_all x0 -> x1, starting transfers between devices: none -> 5.49 us  [body(): blocks = lax.all_to_all(blocks, 'pcol', split_axis=0, concat_axis=0)]
where the time goes in v1:
time: 512 us; the launch traced here: 507 us
  waiting for transfers between devices  310 us (61%)
  blocking collectives  143 us (28%)
  matrix products  36.4 us (7%)
  local copies, waits for them, and re-layouts  12.8 us (2%)
  starting transfers between devices  5.49 us (1%)
    all_to_all x1, waiting for transfers between devices, body(): blocks = lax.all_to_all(blocks, 'pcol', split_axis=0, concat_axis=0)  310 us
    all_to_all x1, blocking collectives, body(): lax.all_to_all(eigen_rows, 'prow', split_axis=1, concat_axis=0, tiled=True)  101 us
    dot_general x6, matrix products, matmul(): jnp.dot(left, right, precision=precision, preferred_element_type=jnp.floa...  36.4 us
    all_to_all x1, blocking collectives, sum_over_prow(): lax.all_to_all(slices, 'prow', split_axis=0, concat_axis=0, tiled=True)  22.4 us
    all_to_all x1, blocking collectives, sum_over_prow(): lax.all_to_all(copies, 'prow', split_axis=0, concat_axis=0, tiled=True)  18.8 us
  transfers between devices with their start and end apart: 1, of which 1 were waited for; matrix products, arithmetic and copies ran while one was open for 0% of the time, Pallas kernels for 0%

profile of v1, /device:TPU:32, one launch (start us, length us, event | category | flops | bytes accessed | tf_op | source)
XLA Modules:
  0.0 507.3 jit_solution(14790434998226724096)
XLA Ops:
  0.0 0.0 copy-start.1
  0.0 101.5 %all_to_all.34 = f32[4,32,7168]{2,0,1:T(4,128)} all-to-all(f32[4,32,7168]{2,0,1:T(4,128)} %bitcast.22), channel_id=1, replica_groups=mesh['prow'=32,'pcol'=8] {'prow'}, dimensions={1} | all-to-all | bytes 7340032 | tf_op jit(solution)/shard_map/all_to_all | solution.py:33
  101.5 0.0 copy-done.1
  101.5 6.9 %stack.2 = f32[8,7168,64]{1,2,0:T(8,128)} broadcast(f32[7168,64]{0,1:T(8,128)S(1)} %copy-done.1), dimensions={1,2} | broadcast | bytes 16515072 | tf_op jit(solution)/shard_map/stack | solution.py:30
  108.5 5.5 %all-to-all-start.1 = ((f32[8,7168,64]{1,2,0:T(8,128)}), f32[8,7168,64]{1,2,0:T(8,128)}, u32[]{:S(2)}, u32[]{:S(2)}) async-start(f32[8,7168,64]{1,2,0:T(8,128)} %stack.2), calls=%async_computation.1 | async-start | bytes 29360128 | tf_op jit(solution)/shard_map/all_to_all | solution.py:31
  113.9 5.2 %all_to_all.26 = f32[128,7168]{1,0:T(8,128)} reshape(f32[32,4,7168]{2,1,0:T(4,128)} %bitcast.21) | data formatting | bytes 7340032 | tf_op jit(solution)/shard_map/all_to_all | solution.py:33
  119.2 309.7 %all-to-all-done.1 = f32[8,7168,64]{1,2,0:T(8,128)} async-done(((f32[8,7168,64]{1,2,0:T(8,128)}), f32[8,7168,64]{1,2,0:T(8,128)}, u32[]{:S(2)}, u32[]{:S(2)}) %all-to-all-start.1) | async-done | bytes 14680096 | tf_op jit(solution)/shard_map/all_to_all | solution.py:31
  428.9 0.0 copy-start
  428.9 11.9 %fusion = f32[256,256]{1,0:T(8,128)S(1)} fusion(f32[7168,512]{0,1:T(8,128)} %bitcast.3), kind=kOutput, calls=%fused_computation.1 | convolution fusion | flops 2818572288 | bytes 14942208 | tf_op jit(solution)/shard_map/dot_general | solution.py:15
  440.7 0.0 copy-done
  440.8 10.7 %fusion.17 = f32[128,512]{1,0:T(8,128)S(1)} fusion(f32[128,7168]{1,0:T(8,128)S(1)} %copy-done, f32[7168,512]{0,1:T(8,128)} %bitcast.3), kind=kOutput, calls=%fused_computation.24 | convolution fusion | flops 2818572288 | bytes 18612224 | tf_op jit(solution)/shard_map/dot_general | solution.py:15
  451.5 0.0 copy-start.2
  451.6 0.1 pad_maximum_fusion
  451.6 22.4 %all_to_all.35 = f32[32,32,128]{2,1,0:T(8,128)S(1)} all-to-all(f32[32,32,128]{2,1,0:T(8,128)S(1)} %pad_maximum_fusion), channel_id=1, replica_groups=mesh['prow'=32,'pcol'=8] {'prow'}, dimensions={0} | all-to-all | bytes 1048576 | tf_op jit(solution)/shard_map/all_to_all | solution.py:20
  474.1 0.1 broadcast_in_dim.2
  474.1 18.8 %all_to_all.36 = f32[32,32,128]{2,1,0:T(8,128)S(1)} all-to-all(f32[32,32,128]{2,1,0:T(8,128)S(1)} %broadcast_in_dim.2), channel_id=1, replica_groups=mesh['prow'=32,'pcol'=8] {'prow'}, dimensions={0} | all-to-all | bytes 1048576 | tf_op jit(solution)/shard_map/all_to_all | solution.py:23
  492.9 0.3 copy.9
  493.3 0.1 reshape.31
  493.4 0.0 copy-done.2
  493.4 0.4 fusion.7
  493.8 0.3 convolution_subtract_fusion.1
  494.1 0.4 fusion.6
  494.5 12.8 %convolution_subtract_fusion = f32[128,7168]{1,0:T(8,128)} fusion(f32[128,7168]{1,0:T(8,128)} %all_to_all.26, f32[7168,512]{0,1:T(8,128)} %bitcast.3, f32[128,256]{1,0:T(8,128)S(1)} %fusion.7, f32[128,256]{1,0:T(8,128)S(1)} %fusion.6), kind=kOutput, calls=%fused_computation | convolution fusion | flops 2819555328 | bytes 22282240 | tf_op jit(solution)/shard_map/dot_general | solution.py:15
  (5 shorter events, 0.2 us)
Async XLA Ops:
  0.0 101.5 %copy-start.1 = (f32[7168,64]{0,1:T(8,128)S(1)}, f32[7168,64]{0,1:T(8,128)}, u32[]{:S(2)}) copy-start(f32[7168,64]{0,1:T(8,128)} %param.4) | copy-start | bytes 5505028
  108.5 320.4 %all-to-all-start.1 = ((f32[8,7168,64]{1,2,0:T(8,128)}), f32[8,7168,64]{1,2,0:T(8,128)}, u32[]{:S(2)}, u32[]{:S(2)}) async-start(f32[8,7168,64]{1,2,0:T(8,128)} %stack.2), calls=%async_computation.1 | async-start | bytes 29360128 | tf_op jit(solution)/shard_map/all_to_all | solution.py:31
  428.9 11.9 %copy-start = (f32[128,7168]{1,0:T(8,128)S(1)}, f32[128,7168]{1,0:T(8,128)}, u32[]{:S(2)}) copy-start(f32[128,7168]{1,0:T(8,128)} %all_to_all.26) | copy-start | bytes 11010052
  451.5 41.9 %copy-start.2 = (f32[2,256,256]{2,1,0:T(8,128)S(1)}, f32[2,256,256]{2,1,0:T(8,128)}, u32[]{:S(2)}) copy-start(f32[2,256,256]{2,1,0:T(8,128)} %param.5) | copy-start | bytes 1572868
